TPU v7x, 128 devices: a whole 4x4x4 slice. The times are simulated.
128 devices in a mesh: pix: 32 (over y, z, core), freq: 4 (over x).
Axes of the slice: x: 4, y: 4, z: 4, core: 2. Of those that a mesh axis runs over, the one named last changes fastest.
Arguments:
- cube: float32 [1024, 65536], P('freq', 'pix'), may hold values from -6 to 6
- probes: float32 [32, 65536], P(None, 'pix'), may hold values from -6 to 6
- galaxy: float32 [65536], P('pix'), may hold values from -6 to 6
- slices: int32 [65536], P('pix'), may hold values from 0 to 127
- valid: int32 [65536], P('pix'), may hold values 0 or 1
Outputs:
- cleaned: float32 [1024, 65536], P('freq', 'pix')
- cross: float32 [1024, 128], P('freq')
All inputs are finite; a program needn't handle non-finite values. No bound on the sum of `valid` on one device may be relied on, other than what follows from the above.
Results may differ from a plain program's by a relative error of at most 0.00019.
Values sent between devices are 32-bit elements; how exact they have to be, the bound alone decides.
No kernel may reach another device: no remote copies, remote signals or barrier semaphores. Data moves between devices by JAX's collectives and lax.ppermute only.
A program may use at most 64 MiB of HBM per device.

v0:
```python
import jax
import jax.numpy as jnp
from jax import lax
from jax.sharding import PartitionSpec as P

NS = 128
ITERS = 4


def prefix(value, axis, join, neutral):
    count, mine = (lax.axis_size(axis), lax.axis_index(axis))
    pieces = lax.all_gather(value, axis)
    total = jnp.full_like(value, 0) + jnp.asarray(neutral, value.dtype)

    def lap(position, total):
        longer = join(total, pieces[position])
        return jnp.where(position < mine, longer, total)

    return lax.fori_loop(0, count - 1, lap, total)


def broadcast(value, axis, source):
    kept = jnp.where(lax.axis_index(axis) == source, value, 0).astype(value.dtype)
    return lax.psum(kept, axis)


def multiply(left, right):
    return jnp.dot(left, right, precision=lax.Precision.HIGHEST, preferred_element_type=jnp.float32)


def orthonormal(factor):
    gram = multiply(factor.T, factor)
    lower = jnp.linalg.cholesky(gram)
    return lax.linalg.triangular_solve(lower, factor, left_side=False, lower=True, transpose_a=True)


def combine_add(earlier, later):
    return earlier + later


def total_pix(term):
    before = prefix(term, "pix", combine_add, jnp.zeros_like(term))
    return broadcast(before + term, "pix", lax.axis_size("pix") - 1)


def fold_freq(term):
    return lax.psum_scatter(term, "freq", scatter_dimension=0, tiled=True)


def gather_rows(term):
    return lax.all_gather(term, "freq", axis=0, tiled=True)


def slice_table(slices, weights):
    levels = jnp.arange(NS, dtype=jnp.int32)
    return (slices[:, None] == levels[None, :]).astype(jnp.float32) * weights[:, None]


def body(cube, probes, galaxy, slices, valid):
    pixels = lax.axis_size("pix") * cube.shape[1]
    factor_scale = (float(pixels) / float(NS)) ** (-0.5)
    weights = galaxy * valid.astype(jnp.float32)
    own = lax.axis_index("freq")
    local = lax.all_to_all(cube, "freq", split_axis=1, concat_axis=0, tiled=True)
    width = local.shape[1]
    start = own * width
    probe_cols = lax.dynamic_slice_in_dim(probes, start, width, 1)
    own_weights = lax.dynamic_slice_in_dim(weights, start, width, 0)
    own_slices = lax.dynamic_slice_in_dim(slices, start, width, 0)
    basis = orthonormal(gather_rows(total_pix(fold_freq(multiply(local, probe_cols.T)))))
    for step in range(ITERS):
        amps = multiply(basis.T, local)
        basis = orthonormal(gather_rows(total_pix(fold_freq(multiply(local, amps.T)))))
    amps = multiply(basis.T, local)
    cleaned_local = local - multiply(basis, amps)
    table = slice_table(own_slices, own_weights)
    cross = total_pix(fold_freq(multiply(cleaned_local, table))) * factor_scale
    cleaned = lax.all_to_all(cleaned_local, "freq", split_axis=0, concat_axis=1, tiled=True)
    return (cleaned, cross)


def solution(mesh):
    in_specs = (P("freq", "pix"), P(None, "pix"), P("pix"), P("pix"), P("pix"))
    out_specs = (P("freq", "pix"), P("freq", None))
    return jax.shard_map(body, mesh=mesh, in_specs=in_specs, out_specs=out_specs, check_vma=False)
```

profile of v0, /device:TPU:1, one launch (start us, length us, event | category | flops | bytes accessed | tf_op | source)
XLA Modules:
  0.0 1482.5 jit_solution(6170851042177497390)
XLA Ops:
  7.2 3.2 copy.32
  10.4 4.8 all-to-all-start
  15.2 25.5 %all-to-all-done = f32[256,4,512]{2,0,1:T(8,128)S(1)} async-done(((f32[256,4,512]{2,0,1:T(8,128)}), f32[256,4,512]{2,0,1:T(8,128)S(1)}, u32[]{:S(2)}, u32[]{:S(2)}) %all-to-all-start) | async-done | bytes 2097184 | tf_op jit(solution)/shard_map/all_to_all | solution.py:64
  40.7 2.7 convolution_bitcast_fusion.9
  43.4 20.1 %reduce-scatter.7.cloned.1.call-done = f32[256,32]{0,1:T(8,128)} async-done(((f32[1024,32]{0,1:T(8,128)}), f32[256,32]{0,1:T(8,128)}) %reduce-scatter.7.cloned.1.call-update) | async-done | bytes 32784 | tf_op jit(solution)/shard_map/reduce_scatter | solution.py:47
  63.6 47.6 %all-gather.13.cloned.1.call-done = f32[8192,32]{0,1:T(8,128)} async-done(((f32[256,32]{0,1:T(8,128)}), f32[8192,32]{0,1:T(8,128)}) %all-gather.13.cloned.1.call-update) | async-done | bytes 1048592 | tf_op jit(solution)/shard_map/all_gather | solution.py:12
  111.1 3.6 copy.24
  114.7 30.1 %while.84 = (s32[]{:T(128)}, f32[256,32]{1,0:T(8,128)S(1)}, s32[]{:T(128)}, f32[32,256,32]{2,1,0:T(8,128)}, s32[]{:T(128)}, /*index=5*/s32[]{:T(128)}) while((s32[]{:T(128)}, f32[256,32]{1,0:T(8,128)S(1)}, s32[]{:T(128)}, f32[32,256,32]{2,1,0:T(8,128)}, s32[]{:T(128)}, /*index=5*/s32[]{:T(128)}) %tuple.222), condition=%wide.region_2.3_spmd.clone, body=%wide.region_1.2_spmd.clone.sunk | while | flops 24580 | bytes 98397 | solution.py:19
  144.9 120.9 %psum.42 = f32[256,32]{0,1:T(8,128)S(1)} all-reduce(f32[256,32]{0,1:T(8,128)S(1)} %add_select_fusion.11), channel_id=1, replica_groups=mesh['pix'=32,'freq'=4] {'pix'}, use_global_device_ids=true, to_apply=%region_3.4 | all-reduce | flops 8192 | bytes 65536 | tf_op jit(solution)/shard_map/psum | solution.py:24
  265.7 9.7 all_gather.53
  275.8 2.9 cholesky.89
  280.0 2.4 custom-call.15
  282.8 1.3 fusion.32
  284.1 2.7 convolution_bitcast_fusion.7
  286.8 21.6 %reduce-scatter.9.cloned.1.call-done = f32[256,32]{0,1:T(8,128)} async-done(((f32[1024,32]{0,1:T(8,128)}), f32[256,32]{0,1:T(8,128)}) %reduce-scatter.9.cloned.1.call-update) | async-done | bytes 32784 | tf_op jit(solution)/shard_map/reduce_scatter | solution.py:47
  308.6 47.4 %all-gather.15.cloned.1.call-done = f32[8192,32]{0,1:T(8,128)} async-done(((f32[256,32]{0,1:T(8,128)}), f32[8192,32]{0,1:T(8,128)}) %all-gather.15.cloned.1.call-update) | async-done | bytes 1048592 | tf_op jit(solution)/shard_map/all_gather | solution.py:12
  356.0 3.6 copy.25
  359.5 30.1 %while.85 = (s32[]{:T(128)}, f32[256,32]{1,0:T(8,128)S(1)}, s32[]{:T(128)}, f32[32,256,32]{2,1,0:T(8,128)}, s32[]{:T(128)}, /*index=5*/s32[]{:T(128)}) while((s32[]{:T(128)}, f32[256,32]{1,0:T(8,128)S(1)}, s32[]{:T(128)}, f32[32,256,32]{2,1,0:T(8,128)}, s32[]{:T(128)}, /*index=5*/s32[]{:T(128)}) %tuple.223), condition=%wide.region_8.11_spmd.clone, body=%wide.region_7.10_spmd.clone.sunk | while | flops 24580 | bytes 98397 | solution.py:19
  389.7 120.9 %psum.43 = f32[256,32]{0,1:T(8,128)S(1)} all-reduce(f32[256,32]{0,1:T(8,128)S(1)} %add_select_fusion.10), channel_id=1, replica_groups=mesh['pix'=32,'freq'=4] {'pix'}, use_global_device_ids=true, to_apply=%region_9.12 | all-reduce | flops 8192 | bytes 65536 | tf_op jit(solution)/shard_map/psum | solution.py:24
  510.6 9.7 all_gather.56
  520.6 2.9 cholesky.100
  524.8 2.4 custom-call.16
  527.6 1.3 fusion.34
  528.9 2.7 convolution_bitcast_fusion.5
  531.7 21.6 %reduce-scatter.11.cloned.1.call-done = f32[256,32]{0,1:T(8,128)} async-done(((f32[1024,32]{0,1:T(8,128)}), f32[256,32]{0,1:T(8,128)}) %reduce-scatter.11.cloned.1.call-update) | async-done | bytes 32784 | tf_op jit(solution)/shard_map/reduce_scatter | solution.py:47
  553.4 47.4 %all-gather.17.cloned.1.call-done = f32[8192,32]{0,1:T(8,128)} async-done(((f32[256,32]{0,1:T(8,128)}), f32[8192,32]{0,1:T(8,128)}) %all-gather.17.cloned.1.call-update) | async-done | bytes 1048592 | tf_op jit(solution)/shard_map/all_gather | solution.py:12
  600.8 3.6 copy.26
  604.4 30.1 %while.86 = (s32[]{:T(128)}, f32[256,32]{1,0:T(8,128)S(1)}, s32[]{:T(128)}, f32[32,256,32]{2,1,0:T(8,128)}, s32[]{:T(128)}, /*index=5*/s32[]{:T(128)}) while((s32[]{:T(128)}, f32[256,32]{1,0:T(8,128)S(1)}, s32[]{:T(128)}, f32[32,256,32]{2,1,0:T(8,128)}, s32[]{:T(128)}, /*index=5*/s32[]{:T(128)}) %tuple.224), condition=%wide.region_12.15_spmd.clone, body=%wide.region_11.14_spmd.clone.sunk | while | flops 24580 | bytes 98397 | solution.py:19
  634.5 120.9 %psum.44 = f32[256,32]{0,1:T(8,128)S(1)} all-reduce(f32[256,32]{0,1:T(8,128)S(1)} %add_select_fusion.9), channel_id=1, replica_groups=mesh['pix'=32,'freq'=4] {'pix'}, use_global_device_ids=true, to_apply=%region_13.16 | all-reduce | flops 8192 | bytes 65536 | tf_op jit(solution)/shard_map/psum | solution.py:24
  755.4 9.9 all_gather.59
  765.6 2.9 cholesky.111
  769.8 2.4 custom-call.17
  772.6 1.3 fusion.36
  773.9 2.7 convolution_bitcast_fusion.3
  776.7 21.7 %reduce-scatter.13.cloned.1.call-done = f32[256,32]{0,1:T(8,128)} async-done(((f32[1024,32]{0,1:T(8,128)}), f32[256,32]{0,1:T(8,128)}) %reduce-scatter.13.cloned.1.call-update) | async-done | bytes 32784 | tf_op jit(solution)/shard_map/reduce_scatter | solution.py:47
  798.4 47.5 %all-gather.19.cloned.1.call-done = f32[8192,32]{0,1:T(8,128)} async-done(((f32[256,32]{0,1:T(8,128)}), f32[8192,32]{0,1:T(8,128)}) %all-gather.19.cloned.1.call-update) | async-done | bytes 1048592 | tf_op jit(solution)/shard_map/all_gather | solution.py:12
  845.9 3.6 copy.27
  849.5 30.1 %while.87 = (s32[]{:T(128)}, f32[256,32]{1,0:T(8,128)S(1)}, s32[]{:T(128)}, f32[32,256,32]{2,1,0:T(8,128)}, s32[]{:T(128)}, /*index=5*/s32[]{:T(128)}) while((s32[]{:T(128)}, f32[256,32]{1,0:T(8,128)S(1)}, s32[]{:T(128)}, f32[32,256,32]{2,1,0:T(8,128)}, s32[]{:T(128)}, /*index=5*/s32[]{:T(128)}) %tuple.225), condition=%wide.region_16.19_spmd.clone, body=%wide.region_15.18_spmd.clone.sunk | while | flops 24580 | bytes 98397 | solution.py:19
  849.5 0.9 add_select_fusion.21
  879.6 120.9 %psum.45 = f32[256,32]{0,1:T(8,128)S(1)} all-reduce(f32[256,32]{0,1:T(8,128)S(1)} %add_select_fusion.8), channel_id=1, replica_groups=mesh['pix'=32,'freq'=4] {'pix'}, use_global_device_ids=true, to_apply=%region_17.20 | all-reduce | flops 8192 | bytes 65536 | tf_op jit(solution)/shard_map/psum | solution.py:24
  1000.5 9.7 all_gather.62
  1010.5 2.9 cholesky.122
  1014.8 2.4 custom-call.18
  1017.6 1.3 fusion.38
  1018.9 2.7 convolution_bitcast_fusion.1
  1021.6 21.6 %reduce-scatter.15.cloned.1.call-done = f32[256,32]{0,1:T(8,128)} async-done(((f32[1024,32]{0,1:T(8,128)}), f32[256,32]{0,1:T(8,128)}) %reduce-scatter.15.cloned.1.call-update) | async-done | bytes 32784 | tf_op jit(solution)/shard_map/reduce_scatter | solution.py:47
  1044.9 45.8 %all-gather.21.cloned.1.call-done = f32[8192,32]{0,1:T(8,128)} async-done(((f32[256,32]{0,1:T(8,128)}), f32[8192,32]{0,1:T(8,128)}) %all-gather.21.cloned.1.call-update) | async-done | bytes 1048592 | tf_op jit(solution)/shard_map/all_gather | solution.py:12
  1090.7 3.6 copy.28
  1094.3 30.1 %while.88 = (s32[]{:T(128)}, f32[256,32]{1,0:T(8,128)S(1)}, s32[]{:T(128)}, f32[32,256,32]{2,1,0:T(8,128)}, s32[]{:T(128)}, /*index=5*/s32[]{:T(128)}) while((s32[]{:T(128)}, f32[256,32]{1,0:T(8,128)S(1)}, s32[]{:T(128)}, f32[32,256,32]{2,1,0:T(8,128)}, s32[]{:T(128)}, /*index=5*/s32[]{:T(128)}) %tuple.226), condition=%wide.region_20.23_spmd.clone, body=%wide.region_19.22_spmd.clone.sunk | while | flops 24580 | bytes 98397 | solution.py:19
  1124.4 120.9 %psum.46 = f32[256,32]{0,1:T(8,128)S(1)} all-reduce(f32[256,32]{0,1:T(8,128)S(1)} %add_select_fusion.7), channel_id=1, replica_groups=mesh['pix'=32,'freq'=4] {'pix'}, use_global_device_ids=true, to_apply=%region_21.24 | all-reduce | flops 8192 | bytes 65536 | tf_op jit(solution)/shard_map/psum | solution.py:24
  1245.3 9.9 all_gather.65
  1255.6 2.9 cholesky.133
  1259.8 2.4 custom-call.19
  1262.6 1.3 fusion.40
  1263.9 1.8 convolution_subtract_fusion
  1265.8 1.3 copy-done.1
  1267.1 2.7 fusion
  1269.8 22.6 %reduce-scatter.17.cloned.1.call-done = f32[256,128]{1,0:T(8,128)} async-done(((f32[1024,128]{1,0:T(8,128)}), f32[256,128]{1,0:T(8,128)}) %reduce-scatter.17.cloned.1.call-update) | async-done | bytes 131088 | tf_op jit(solution)/shard_map/reduce_scatter | solution.py:47
  1292.4 3.6 all-to-all-start.1
  1296.1 47.1 %all-gather.23.cloned.1.call-done = f32[8192,128]{1,0:T(8,128)} async-done(((f32[256,128]{1,0:T(8,128)}), f32[8192,128]{1,0:T(8,128)}) %all-gather.23.cloned.1.call-update) | async-done | bytes 4194320 | tf_op jit(solution)/shard_map/all_gather | solution.py:12
  1343.3 30.0 %while.89 = (s32[]{:T(128)}, f32[256,128]{1,0:T(8,128)S(1)}, s32[]{:T(128)}, f32[32,256,128]{2,1,0:T(8,128)}, s32[]{:T(128)}, /*index=5*/s32[]{:T(128)}) while((s32[]{:T(128)}, f32[256,128]{1,0:T(8,128)S(1)}, s32[]{:T(128)}, f32[32,256,128]{2,1,0:T(8,128)}, s32[]{:T(128)}, /*index=5*/s32[]{:T(128)}) %tuple.227), condition=%wide.region_24.27_spmd.clone, body=%wide.region_23.26_spmd.clone.sunk | while | flops 98308 | bytes 393309 | solution.py:19
  1374.0 1.6 copy.30
  1375.6 98.8 %all-reduce.2.cloned.1.call-done = f32[256,128]{1,0:T(8,128)} async-done(((f32[256,128]{1,0:T(8,128)}), f32[256,128]{1,0:T(8,128)}) %all-reduce.2.cloned.1.call-update) | async-done | bytes 131088 | tf_op jit(solution)/shard_map/psum | solution.py:24
  1474.4 1.6 broadcast_multiply_fusion
  (281 shorter events, 188.6 us)
Async XLA Ops:
  7.2 33.5 %copy-start = (f32[32,2048]{1,0:T(8,128)S(1)}, f32[32,2048]{1,0:T(8,128)}, u32[]{:S(2)}) copy-start(f32[32,2048]{1,0:T(8,128)} %param.21) | copy-start | bytes 786436
  10.4 30.3 %all-to-all-start = ((f32[256,4,512]{2,0,1:T(8,128)}), f32[256,4,512]{2,0,1:T(8,128)S(1)}, u32[]{:S(2)}, u32[]{:S(2)}) async-start(f32[256,4,512]{2,0,1:T(8,128)} %bitcast.156), calls=%async_computation | async-start | bytes 4194304 | tf_op jit(solution)/shard_map/all_to_all | solution.py:64
  15.2 48.3 %reduce-scatter.7.cloned.1.call-start = ((), (), s32[]{:S(2)}) async-start(), calls=%async_computation.8 | async-start | bytes 163840 | tf_op jit(solution)/shard_map/reduce_scatter | solution.py:47
  43.4 67.8 %all-gather.13.cloned.1.call-start = ((), (), s32[]{:S(2)}) async-start(), calls=%async_computation.15 | async-start | bytes 1081344 | tf_op jit(solution)/shard_map/all_gather | solution.py:12
  63.5 245.0 %reduce-scatter.9.cloned.1.call-start = ((), (), s32[]{:S(2)}) async-start(), calls=%async_computation.9 | async-start | bytes 163840 | tf_op jit(solution)/shard_map/reduce_scatter | solution.py:47
  114.7 30.1 %copy-start.3 = (f32[256,32]{0,1:T(8,128)S(1)}, f32[256,32]{0,1:T(8,128)}, u32[]{:S(2)}) copy-start(f32[256,32]{0,1:T(8,128)} %reduce-scatter.7.cloned.1.call-done) | copy-start | bytes 98308
  286.8 69.2 %all-gather.15.cloned.1.call-start = ((), (), s32[]{:S(2)}) async-start(), calls=%async_computation.16 | async-start | bytes 1081344 | tf_op jit(solution)/shard_map/all_gather | solution.py:12
  308.5 244.8 %reduce-scatter.11.cloned.1.call-start = ((), (), s32[]{:S(2)}) async-start(), calls=%async_computation.10 | async-start | bytes 163840 | tf_op jit(solution)/shard_map/reduce_scatter | solution.py:47
  359.5 30.1 %copy-start.5 = (f32[256,32]{0,1:T(8,128)S(1)}, f32[256,32]{0,1:T(8,128)}, u32[]{:S(2)}) copy-start(f32[256,32]{0,1:T(8,128)} %reduce-scatter.9.cloned.1.call-done) | copy-start | bytes 98308
  531.6 69.2 %all-gather.17.cloned.1.call-start = ((), (), s32[]{:S(2)}) async-start(), calls=%async_computation.17 | async-start | bytes 1081344 | tf_op jit(solution)/shard_map/all_gather | solution.py:12
  553.3 245.0 %reduce-scatter.13.cloned.1.call-start = ((), (), s32[]{:S(2)}) async-start(), calls=%async_computation.11 | async-start | bytes 163840 | tf_op jit(solution)/shard_map/reduce_scatter | solution.py:47
  604.3 30.1 %copy-start.6 = (f32[256,32]{0,1:T(8,128)S(1)}, f32[256,32]{0,1:T(8,128)}, u32[]{:S(2)}) copy-start(f32[256,32]{0,1:T(8,128)} %reduce-scatter.11.cloned.1.call-done) | copy-start | bytes 98308
  776.6 69.3 %all-gather.19.cloned.1.call-start = ((), (), s32[]{:S(2)}) async-start(), calls=%async_computation.18 | async-start | bytes 1081344 | tf_op jit(solution)/shard_map/all_gather | solution.py:12
  798.3 244.9 %reduce-scatter.15.cloned.1.call-start = ((), (), s32[]{:S(2)}) async-start(), calls=%async_computation.12 | async-start | bytes 163840 | tf_op jit(solution)/shard_map/reduce_scatter | solution.py:47
  849.5 30.1 %copy-start.7 = (f32[256,32]{0,1:T(8,128)S(1)}, f32[256,32]{0,1:T(8,128)}, u32[]{:S(2)}) copy-start(f32[256,32]{0,1:T(8,128)} %reduce-scatter.13.cloned.1.call-done) | copy-start | bytes 98308
  1021.6 69.1 %all-gather.21.cloned.1.call-start = ((), (), s32[]{:S(2)}) async-start(), calls=%async_computation.19 | async-start | bytes 1081344 | tf_op jit(solution)/shard_map/all_gather | solution.py:12
  1043.3 249.1 %reduce-scatter.17.cloned.1.call-start = ((), (), s32[]{:S(2)}) async-start(), calls=%async_computation.13 | async-start | bytes 655360 | tf_op jit(solution)/shard_map/reduce_scatter | solution.py:47
  1094.3 30.1 %copy-start.4 = (f32[256,32]{0,1:T(8,128)S(1)}, f32[256,32]{0,1:T(8,128)}, u32[]{:S(2)}) copy-start(f32[256,32]{0,1:T(8,128)} %reduce-scatter.15.cloned.1.call-done) | copy-start | bytes 98308
  1265.7 1.3 copy-start.1
  1269.8 73.5 %all-gather.23.cloned.1.call-start = ((), (), s32[]{:S(2)}) async-start(), calls=%async_computation.20 | async-start | bytes 4325376 | tf_op jit(solution)/shard_map/all_gather | solution.py:12
  1292.4 81.6 %all-to-all-start.1 = ((f32[4,256,512]{2,1,0:T(8,128)}), f32[4,256,512]{2,1,0:T(8,128)S(1)}, u32[]{:S(2)}, u32[]{:S(2)}) async-start(f32[4,256,512]{2,1,0:T(8,128)} %bitcast.154), calls=%async_computation.6 | async-start | bytes 4194304 | tf_op jit(solution)/shard_map/all_to_all | solution.py:78
  1296.1 77.2 %copy-start.2 = (f32[256,128]{1,0:T(8,128)S(1)}, f32[256,128]{1,0:T(8,128)}, u32[]{:S(2)}) copy-start(f32[256,128]{1,0:T(8,128)} %reduce-scatter.17.cloned.1.call-done) | copy-start | bytes 393220
  1296.1 178.3 %all-reduce.2.cloned.1.call-start = ((), (), s32[]{:S(2)}) async-start(), calls=%async_computation.14 | async-start | bytes 262144 | tf_op jit(solution)/shard_map/psum | solution.py:24
Sparse Core Ops, SparseCore 0:
  43.5 19.9 reduce-scatter.6
  65.7 45.4 all-gather.12
  286.9 21.5 reduce-scatter.8
  310.5 45.4 all-gather.14
  531.7 21.5 reduce-scatter.10
  555.3 45.4 all-gather.16
  776.7 21.5 reduce-scatter.12
  800.5 45.3 all-gather.18
  1021.7 21.5 reduce-scatter.14
  1045.3 45.3 all-gather.20
  1269.9 22.4 reduce-scatter.16
  1294.5 48.6 all-gather.22
  1374.1 100.2 all-reduce.1
where the time goes:
time: 1490 us; the launch traced here: 1480 us
  blocking collectives  653 us (44%)
  waiting for transfers between devices  537 us (36%)
  other arithmetic  213 us (14%)
  matrix products  27.3 us (2%)
  local copies, waits for them, and re-layouts  25.4 us (2%)
    psum x5, blocking collectives, broadcast(): return lax.psum(kept, axis)  604 us
    all_gather x6, waiting for transfers between devices, prefix(): pieces = lax.all_gather(value, axis)  283 us
    select_n x186, other arithmetic, lap(): return jnp.where(position < mine, longer, total)  176 us
    reduce_scatter x6, waiting for transfers between devices, fold_freq(): return lax.psum_scatter(term, 'freq', scatter_dimension=0, tiled=True)  129 us
    psum x1, waiting for transfers between devices, broadcast(): return lax.psum(kept, axis)  98.8 us
    all_gather x5, blocking collectives, gather_rows(): return lax.all_gather(term, 'freq', axis=0, tiled=True)  48.9 us
  transfers between devices with their start and end apart: 15, of which 14 were waited for; matrix products, arithmetic and copies ran while one was open for 2% of the time, Pallas kernels for 0%

commit v1 on v0

--- a/solution.py
+++ b/solution.py
@@ -21,7 +21,7 @@
 
 def broadcast(value, axis, source):
     kept = jnp.where(lax.axis_index(axis) == source, value, 0).astype(value.dtype)
-    return lax.psum(kept, axis)
+    return jnp.sum(lax.all_gather(kept, axis), axis=0)
 
 
 def multiply(left, right):

time: 1490 us -> 1040 us (0.70)
  blocking collectives: 653 us -> 79.2 us
  waiting for transfers between devices: 537 us -> 656 us
    psum x5 -> x0, blocking collectives: 604 us -> none  [broadcast(): return lax.psum(kept, axis)]
    all_gather x0 -> x6, waiting for transfers between devices: none -> 224 us  [broadcast(): return jnp.sum(lax.all_gather(kept, axis), axis=0)]
    psum x1 -> x0, waiting for transfers between devices: 98.8 us -> none  [broadcast(): return lax.psum(kept, axis)]
    all_to_all x0 -> x1, blocking collectives: none -> 29.8 us  [body(): lax.all_to_all(cleaned_local, 'freq', split_axis=0, concat_axis=1, tiled=...]
  transfers between devices with their start and end apart: 15 -> 19, of which waited for: 14 -> 19; matrix products, arithmetic and copies ran while one was open for 2% -> 0% of each run, Pallas kernels for 0% -> 0%
where the time goes in v1:
time: 1040 us
  waiting for transfers between devices  656 us (63%)
  other arithmetic  218 us (21%)
  blocking collectives  79.2 us (8%)
  local copies, waits for them, and re-layouts  33.2 us (3%)
  matrix products  27.3 us (3%)
  between operations  14.7 us (1%)
    all_gather x6, waiting for transfers between devices, prefix(): pieces = lax.all_gather(value, axis)  288 us
    all_gather x6, waiting for transfers between devices, broadcast(): return jnp.sum(lax.all_gather(kept, axis), axis=0)  224 us
    select_n x186, other arithmetic, lap(): return jnp.where(position < mine, longer, total)  176 us
    reduce_scatter x6, waiting for transfers between devices, fold_freq(): return lax.psum_scatter(term, 'freq', scatter_dimension=0, tiled=True)  118 us
    all_gather x5, blocking collectives, gather_rows(): return lax.all_gather(term, 'freq', axis=0, tiled=True)  49.4 us
    all_to_all x1, blocking collectives, body(): lax.all_to_all(cleaned_local, 'freq', split_axis=0, concat_axis=1, tiled=...  29.8 us
    unnamed x26, local copies, waits for them, and re-layouts  27 us
    dot_general x17, matrix products, multiply(): jnp.dot(left, right, precision=lax.Precision.HIGHEST, preferred_element_t...  25.6 us
  transfers between devices with their start and end apart: 19, of which 19 were waited for; matrix products, arithmetic and copies ran while one was open for 0% of the time, Pallas kernels for 0%

profile of v1, /device:TPU:1, one launch (start us, length us, event | category | flops | bytes accessed | tf_op | source)
XLA Modules:
  0.0 1037.6 jit_solution(16418420212328314926)
XLA Ops:
  7.2 3.2 copy.54
  10.4 4.8 all-to-all-start
  15.2 25.5 %all-to-all-done = f32[256,4,512]{2,0,1:T(8,128)S(1)} async-done(((f32[256,4,512]{2,0,1:T(8,128)}), f32[256,4,512]{2,0,1:T(8,128)S(1)}, u32[]{:S(2)}, u32[]{:S(2)}) %all-to-all-start) | async-done | bytes 2097184 | tf_op jit(solution)/shard_map/all_to_all | solution.py:64
  40.7 2.7 convolution_bitcast_fusion.9
  43.4 20.1 %reduce-scatter.7.cloned.1.call-done = f32[256,32]{0,1:T(8,128)} async-done(((f32[1024,32]{0,1:T(8,128)}), f32[256,32]{0,1:T(8,128)}) %reduce-scatter.7.cloned.1.call-update) | async-done | bytes 32784 | tf_op jit(solution)/shard_map/reduce_scatter | solution.py:47
  63.6 47.6 %all-gather.25.cloned.1.call-done = f32[8192,32]{0,1:T(8,128)} async-done(((f32[256,32]{0,1:T(8,128)}), f32[8192,32]{0,1:T(8,128)}) %all-gather.25.cloned.1.call-update) | async-done | bytes 1048592 | tf_op jit(solution)/shard_map/all_gather | solution.py:12
  111.1 3.6 copy.41
  114.7 30.1 %while.84 = (s32[]{:T(128)}, f32[256,32]{1,0:T(8,128)S(1)}, s32[]{:T(128)}, f32[32,256,32]{2,1,0:T(8,128)}, s32[]{:T(128)}, /*index=5*/s32[]{:T(128)}) while((s32[]{:T(128)}, f32[256,32]{1,0:T(8,128)S(1)}, s32[]{:T(128)}, f32[32,256,32]{2,1,0:T(8,128)}, s32[]{:T(128)}, /*index=5*/s32[]{:T(128)}) %tuple.237), condition=%wide.region_2.3_spmd.clone, body=%wide.region_1.2_spmd.clone.sunk | while | flops 24580 | bytes 98397 | solution.py:19
  145.6 42.3 %all-gather.27.cloned.1.call-done = f32[8192,32]{0,1:T(8,128)} async-done(((f32[256,32]{0,1:T(8,128)}), f32[8192,32]{0,1:T(8,128)}) %all-gather.27.cloned.1.call-update) | async-done | bytes 1048592 | tf_op jit(solution)/shard_map/all_gather | solution.py:24
  187.9 1.5 copy.48
  189.6 9.8 all_gather.91
  199.7 2.9 cholesky.89
  204.0 2.4 custom-call.15
  206.8 1.3 fusion.32
  208.1 2.7 convolution_bitcast_fusion.7
  210.8 19.3 %reduce-scatter.9.cloned.1.call-done = f32[256,32]{0,1:T(8,128)} async-done(((f32[1024,32]{0,1:T(8,128)}), f32[256,32]{0,1:T(8,128)}) %reduce-scatter.9.cloned.1.call-update) | async-done | bytes 32784 | tf_op jit(solution)/shard_map/reduce_scatter | solution.py:47
  230.2 47.4 %all-gather.29.cloned.1.call-done = f32[8192,32]{0,1:T(8,128)} async-done(((f32[256,32]{0,1:T(8,128)}), f32[8192,32]{0,1:T(8,128)}) %all-gather.29.cloned.1.call-update) | async-done | bytes 1048592 | tf_op jit(solution)/shard_map/all_gather | solution.py:12
  277.6 3.6 copy.42
  281.1 30.1 %while.85 = (s32[]{:T(128)}, f32[256,32]{1,0:T(8,128)S(1)}, s32[]{:T(128)}, f32[32,256,32]{2,1,0:T(8,128)}, s32[]{:T(128)}, /*index=5*/s32[]{:T(128)}) while((s32[]{:T(128)}, f32[256,32]{1,0:T(8,128)S(1)}, s32[]{:T(128)}, f32[32,256,32]{2,1,0:T(8,128)}, s32[]{:T(128)}, /*index=5*/s32[]{:T(128)}) %tuple.238), condition=%wide.region_8.11_spmd.clone, body=%wide.region_7.10_spmd.clone.sunk | while | flops 24580 | bytes 98397 | solution.py:19
  312.0 42.3 %all-gather.31.cloned.1.call-done = f32[8192,32]{0,1:T(8,128)} async-done(((f32[256,32]{0,1:T(8,128)}), f32[8192,32]{0,1:T(8,128)}) %all-gather.31.cloned.1.call-update) | async-done | bytes 1048592 | tf_op jit(solution)/shard_map/all_gather | solution.py:24
  354.3 1.5 copy.49
  356.0 9.8 all_gather.96
  366.1 2.9 cholesky.100
  370.4 2.4 custom-call.16
  374.5 2.7 convolution_bitcast_fusion.5
  377.2 19.3 %reduce-scatter.11.cloned.1.call-done = f32[256,32]{0,1:T(8,128)} async-done(((f32[1024,32]{0,1:T(8,128)}), f32[256,32]{0,1:T(8,128)}) %reduce-scatter.11.cloned.1.call-update) | async-done | bytes 32784 | tf_op jit(solution)/shard_map/reduce_scatter | solution.py:47
  396.8 47.3 %all-gather.33.cloned.1.call-done = f32[8192,32]{0,1:T(8,128)} async-done(((f32[256,32]{0,1:T(8,128)}), f32[8192,32]{0,1:T(8,128)}) %all-gather.33.cloned.1.call-update) | async-done | bytes 1048592 | tf_op jit(solution)/shard_map/all_gather | solution.py:12
  444.1 3.6 copy.43
  447.7 30.1 %while.86 = (s32[]{:T(128)}, f32[256,32]{1,0:T(8,128)S(1)}, s32[]{:T(128)}, f32[32,256,32]{2,1,0:T(8,128)}, s32[]{:T(128)}, /*index=5*/s32[]{:T(128)}) while((s32[]{:T(128)}, f32[256,32]{1,0:T(8,128)S(1)}, s32[]{:T(128)}, f32[32,256,32]{2,1,0:T(8,128)}, s32[]{:T(128)}, /*index=5*/s32[]{:T(128)}) %tuple.239), condition=%wide.region_12.15_spmd.clone, body=%wide.region_11.14_spmd.clone.sunk | while | flops 24580 | bytes 98397 | solution.py:19
  478.6 42.3 %all-gather.35.cloned.1.call-done = f32[8192,32]{0,1:T(8,128)} async-done(((f32[256,32]{0,1:T(8,128)}), f32[8192,32]{0,1:T(8,128)}) %all-gather.35.cloned.1.call-update) | async-done | bytes 1048592 | tf_op jit(solution)/shard_map/all_gather | solution.py:24
  520.9 1.5 copy.50
  522.5 9.8 all_gather.101
  532.7 2.9 cholesky.111
  537.0 2.4 custom-call.17
  541.1 2.7 convolution_bitcast_fusion.3
  543.8 19.3 %reduce-scatter.13.cloned.1.call-done = f32[256,32]{0,1:T(8,128)} async-done(((f32[1024,32]{0,1:T(8,128)}), f32[256,32]{0,1:T(8,128)}) %reduce-scatter.13.cloned.1.call-update) | async-done | bytes 32784 | tf_op jit(solution)/shard_map/reduce_scatter | solution.py:47
  563.2 47.5 %all-gather.37.cloned.1.call-done = f32[8192,32]{0,1:T(8,128)} async-done(((f32[256,32]{0,1:T(8,128)}), f32[8192,32]{0,1:T(8,128)}) %all-gather.37.cloned.1.call-update) | async-done | bytes 1048592 | tf_op jit(solution)/shard_map/all_gather | solution.py:12
  610.7 3.6 copy.44
  614.3 30.1 %while.87 = (s32[]{:T(128)}, f32[256,32]{1,0:T(8,128)S(1)}, s32[]{:T(128)}, f32[32,256,32]{2,1,0:T(8,128)}, s32[]{:T(128)}, /*index=5*/s32[]{:T(128)}) while((s32[]{:T(128)}, f32[256,32]{1,0:T(8,128)S(1)}, s32[]{:T(128)}, f32[32,256,32]{2,1,0:T(8,128)}, s32[]{:T(128)}, /*index=5*/s32[]{:T(128)}) %tuple.240), condition=%wide.region_16.19_spmd.clone, body=%wide.region_15.18_spmd.clone.sunk | while | flops 24580 | bytes 98397 | solution.py:19
  645.1 42.3 %all-gather.39.cloned.1.call-done = f32[8192,32]{0,1:T(8,128)} async-done(((f32[256,32]{0,1:T(8,128)}), f32[8192,32]{0,1:T(8,128)}) %all-gather.39.cloned.1.call-update) | async-done | bytes 1048592 | tf_op jit(solution)/shard_map/all_gather | solution.py:24
  687.5 1.5 copy.51
  689.1 9.8 all_gather.106
  699.3 2.9 cholesky.122
  703.5 2.4 custom-call.18
  707.6 2.7 convolution_bitcast_fusion.1
  710.4 19.3 %reduce-scatter.15.cloned.1.call-done = f32[256,32]{0,1:T(8,128)} async-done(((f32[1024,32]{0,1:T(8,128)}), f32[256,32]{0,1:T(8,128)}) %reduce-scatter.15.cloned.1.call-update) | async-done | bytes 32784 | tf_op jit(solution)/shard_map/reduce_scatter | solution.py:47
  729.7 47.4 %all-gather.41.cloned.1.call-done = f32[8192,32]{0,1:T(8,128)} async-done(((f32[256,32]{0,1:T(8,128)}), f32[8192,32]{0,1:T(8,128)}) %all-gather.41.cloned.1.call-update) | async-done | bytes 1048592 | tf_op jit(solution)/shard_map/all_gather | solution.py:12
  777.1 3.6 copy.45
  780.7 30.1 %while.88 = (s32[]{:T(128)}, f32[256,32]{1,0:T(8,128)S(1)}, s32[]{:T(128)}, f32[32,256,32]{2,1,0:T(8,128)}, s32[]{:T(128)}, /*index=5*/s32[]{:T(128)}) while((s32[]{:T(128)}, f32[256,32]{1,0:T(8,128)S(1)}, s32[]{:T(128)}, f32[32,256,32]{2,1,0:T(8,128)}, s32[]{:T(128)}, /*index=5*/s32[]{:T(128)}) %tuple.241), condition=%wide.region_20.23_spmd.clone, body=%wide.region_19.22_spmd.clone.sunk | while | flops 24580 | bytes 98397 | solution.py:19
  813.1 40.8 %all-gather.43.cloned.1.call-done = f32[8192,32]{0,1:T(8,128)} async-done(((f32[256,32]{0,1:T(8,128)}), f32[8192,32]{0,1:T(8,128)}) %all-gather.43.cloned.1.call-update) | async-done | bytes 1048592 | tf_op jit(solution)/shard_map/all_gather | solution.py:24
  853.9 1.5 copy.52
  855.5 10.1 all_gather.111
  865.9 2.9 cholesky.133
  870.2 2.4 custom-call.19
  874.3 1.8 convolution_subtract_fusion
  876.1 1.3 copy-done.1
  877.4 2.7 fusion
  880.2 20.2 %reduce-scatter.17.cloned.1.call-done = f32[256,128]{1,0:T(8,128)} async-done(((f32[1024,128]{1,0:T(8,128)}), f32[256,128]{1,0:T(8,128)}) %reduce-scatter.17.cloned.1.call-update) | async-done | bytes 131088 | tf_op jit(solution)/shard_map/reduce_scatter | solution.py:47
  900.5 50.8 %all-gather.45.cloned.1.call-done = f32[8192,128]{1,0:T(8,128)} async-done(((f32[256,128]{1,0:T(8,128)}), f32[8192,128]{1,0:T(8,128)}) %all-gather.45.cloned.1.call-update) | async-done | bytes 4194320 | tf_op jit(solution)/shard_map/all_gather | solution.py:12
  951.3 30.0 %while.89 = (s32[]{:T(128)}, f32[256,128]{1,0:T(8,128)S(1)}, s32[]{:T(128)}, f32[32,256,128]{2,1,0:T(8,128)}, s32[]{:T(128)}, /*index=5*/s32[]{:T(128)}) while((s32[]{:T(128)}, f32[256,128]{1,0:T(8,128)S(1)}, s32[]{:T(128)}, f32[32,256,128]{2,1,0:T(8,128)}, s32[]{:T(128)}, /*index=5*/s32[]{:T(128)}) %tuple.242), condition=%wide.region_24.27_spmd.clone, body=%wide.region_23.26_spmd.clone.sunk | while | flops 98308 | bytes 393309 | solution.py:19
  982.0 29.8 %all_to_all.38 = f32[4,256,512]{2,1,0:T(8,128)S(1)} all-to-all(f32[4,256,512]{2,1,0:T(8,128)} %bitcast.180), channel_id=1, replica_groups=mesh['pix'=32,'freq'=4] {'freq'}, dimensions={0} | all-to-all | bytes 4194304 | tf_op jit(solution)/shard_map/all_to_all | solution.py:78
  1011.9 1.6 copy.47
  1013.4 14.2 %all-gather.47.cloned.1.call-done = f32[8192,128]{1,0:T(8,128)} async-done(((f32[256,128]{1,0:T(8,128)}), f32[8192,128]{1,0:T(8,128)}) %all-gather.47.cloned.1.call-update) | async-done | bytes 4194320 | tf_op jit(solution)/shard_map/all_gather | solution.py:24
  1027.6 2.4 reduce_sum.59
  (301 shorter events, 199.4 us)
Async XLA Ops:
  7.2 33.5 %copy-start = (f32[32,2048]{1,0:T(8,128)S(1)}, f32[32,2048]{1,0:T(8,128)}, u32[]{:S(2)}) copy-start(f32[32,2048]{1,0:T(8,128)} %param.21) | copy-start | bytes 786436
  10.4 30.3 %all-to-all-start = ((f32[256,4,512]{2,0,1:T(8,128)}), f32[256,4,512]{2,0,1:T(8,128)S(1)}, u32[]{:S(2)}, u32[]{:S(2)}) async-start(f32[256,4,512]{2,0,1:T(8,128)} %bitcast.181), calls=%async_computation | async-start | bytes 4194304 | tf_op jit(solution)/shard_map/all_to_all | solution.py:64
  15.2 48.3 %reduce-scatter.7.cloned.1.call-start = ((), (), s32[]{:S(2)}) async-start(), calls=%async_computation.8 | async-start | bytes 163840 | tf_op jit(solution)/shard_map/reduce_scatter | solution.py:47
  43.4 67.8 %all-gather.25.cloned.1.call-start = ((), (), s32[]{:S(2)}) async-start(), calls=%async_computation.14 | async-start | bytes 1081344 | tf_op jit(solution)/shard_map/all_gather | solution.py:12
  63.5 124.4 %all-gather.27.cloned.1.call-start = ((), (), s32[]{:S(2)}) async-start(), calls=%async_computation.15 | async-start | bytes 1081344 | tf_op jit(solution)/shard_map/all_gather | solution.py:24
  114.7 30.1 %copy-start.3 = (f32[256,32]{0,1:T(8,128)S(1)}, f32[256,32]{0,1:T(8,128)}, u32[]{:S(2)}) copy-start(f32[256,32]{0,1:T(8,128)} %reduce-scatter.7.cloned.1.call-done) | copy-start | bytes 98308
  145.5 84.6 %reduce-scatter.9.cloned.1.call-start = ((), (), s32[]{:S(2)}) async-start(), calls=%async_computation.9 | async-start | bytes 163840 | tf_op jit(solution)/shard_map/reduce_scatter | solution.py:47
  210.8 66.8 %all-gather.29.cloned.1.call-start = ((), (), s32[]{:S(2)}) async-start(), calls=%async_computation.16 | async-start | bytes 1081344 | tf_op jit(solution)/shard_map/all_gather | solution.py:12
  230.1 124.2 %all-gather.31.cloned.1.call-start = ((), (), s32[]{:S(2)}) async-start(), calls=%async_computation.17 | async-start | bytes 1081344 | tf_op jit(solution)/shard_map/all_gather | solution.py:24
  281.1 30.1 %copy-start.4 = (f32[256,32]{0,1:T(8,128)S(1)}, f32[256,32]{0,1:T(8,128)}, u32[]{:S(2)}) copy-start(f32[256,32]{0,1:T(8,128)} %reduce-scatter.9.cloned.1.call-done) | copy-start | bytes 98308
  311.9 84.6 %reduce-scatter.11.cloned.1.call-start = ((), (), s32[]{:S(2)}) async-start(), calls=%async_computation.10 | async-start | bytes 163840 | tf_op jit(solution)/shard_map/reduce_scatter | solution.py:47
  377.2 67.0 %all-gather.33.cloned.1.call-start = ((), (), s32[]{:S(2)}) async-start(), calls=%async_computation.18 | async-start | bytes 1081344 | tf_op jit(solution)/shard_map/all_gather | solution.py:12
  396.5 124.3 %all-gather.35.cloned.1.call-start = ((), (), s32[]{:S(2)}) async-start(), calls=%async_computation.19 | async-start | bytes 1081344 | tf_op jit(solution)/shard_map/all_gather | solution.py:24
  447.7 30.1 %copy-start.5 = (f32[256,32]{0,1:T(8,128)S(1)}, f32[256,32]{0,1:T(8,128)}, u32[]{:S(2)}) copy-start(f32[256,32]{0,1:T(8,128)} %reduce-scatter.11.cloned.1.call-done) | copy-start | bytes 98308
  478.5 84.6 %reduce-scatter.13.cloned.1.call-start = ((), (), s32[]{:S(2)}) async-start(), calls=%async_computation.11 | async-start | bytes 163840 | tf_op jit(solution)/shard_map/reduce_scatter | solution.py:47
  543.7 67.0 %all-gather.37.cloned.1.call-start = ((), (), s32[]{:S(2)}) async-start(), calls=%async_computation.20 | async-start | bytes 1081344 | tf_op jit(solution)/shard_map/all_gather | solution.py:12
  563.1 124.3 %all-gather.39.cloned.1.call-start = ((), (), s32[]{:S(2)}) async-start(), calls=%async_computation.21 | async-start | bytes 1081344 | tf_op jit(solution)/shard_map/all_gather | solution.py:24
  614.3 30.1 %copy-start.6 = (f32[256,32]{0,1:T(8,128)S(1)}, f32[256,32]{0,1:T(8,128)}, u32[]{:S(2)}) copy-start(f32[256,32]{0,1:T(8,128)} %reduce-scatter.13.cloned.1.call-done) | copy-start | bytes 98308
  645.1 84.6 %reduce-scatter.15.cloned.1.call-start = ((), (), s32[]{:S(2)}) async-start(), calls=%async_computation.12 | async-start | bytes 163840 | tf_op jit(solution)/shard_map/reduce_scatter | solution.py:47
  710.3 66.8 %all-gather.41.cloned.1.call-start = ((), (), s32[]{:S(2)}) async-start(), calls=%async_computation.22 | async-start | bytes 1081344 | tf_op jit(solution)/shard_map/all_gather | solution.py:12
  729.7 124.2 %all-gather.43.cloned.1.call-start = ((), (), s32[]{:S(2)}) async-start(), calls=%async_computation.23 | async-start | bytes 1081344 | tf_op jit(solution)/shard_map/all_gather | solution.py:24
  780.7 30.1 %copy-start.7 = (f32[256,32]{0,1:T(8,128)S(1)}, f32[256,32]{0,1:T(8,128)}, u32[]{:S(2)}) copy-start(f32[256,32]{0,1:T(8,128)} %reduce-scatter.15.cloned.1.call-done) | copy-start | bytes 98308
  811.5 88.9 %reduce-scatter.17.cloned.1.call-start = ((), (), s32[]{:S(2)}) async-start(), calls=%async_computation.13 | async-start | bytes 655360 | tf_op jit(solution)/shard_map/reduce_scatter | solution.py:47
  876.1 1.3 copy-start.1
  880.2 71.1 %all-gather.45.cloned.1.call-start = ((), (), s32[]{:S(2)}) async-start(), calls=%async_computation.24 | async-start | bytes 4325376 | tf_op jit(solution)/shard_map/all_gather | solution.py:12
  900.4 80.9 %copy-start.2 = (f32[256,128]{1,0:T(8,128)S(1)}, f32[256,128]{1,0:T(8,128)}, u32[]{:S(2)}) copy-start(f32[256,128]{1,0:T(8,128)} %reduce-scatter.17.cloned.1.call-done) | copy-start | bytes 393220
  900.5 127.2 %all-gather.47.cloned.1.call-start = ((), (), s32[]{:S(2)}) async-start(), calls=%async_computation.25 | async-start | bytes 4325376 | tf_op jit(solution)/shard_map/all_gather | solution.py:24
Sparse Core Ops, SparseCore 0:
  43.5 19.9 reduce-scatter.6
  65.7 45.4 all-gather.24
  145.6 42.2 all-gather.26
  210.9 19.1 reduce-scatter.8
  232.1 45.3 all-gather.28
  312.1 42.2 all-gather.30
  377.3 19.1 reduce-scatter.10
  398.7 45.3 all-gather.32
  478.6 42.2 all-gather.34
  543.9 19.1 reduce-scatter.12
  565.3 45.3 all-gather.36
  645.2 42.2 all-gather.38
  710.4 19.1 reduce-scatter.14
  731.7 45.3 all-gather.40
  811.6 42.2 all-gather.42
  880.3 20.1 reduce-scatter.16
  902.5 48.6 all-gather.44
  982.2 45.4 all-gather.46
